TPU v7x, 32 devices: a whole 2x2x4 slice. The times are simulated.
32 devices in a mesh: wide: 8 (over z, core), narrow: 4 (over y, x).
Axes of the slice: x: 2, y: 2, z: 4, core: 2. Of those that a mesh axis runs over, the one named last changes fastest.
Arguments:
- tokens: bfloat16 [4096, 2048], P('wide'), may hold values from -6 to 6
- attn_gain: bfloat16 [2048], replicated, may hold values from 0.099609375 to 1.8984375
- w_query: bfloat16 [2048, 2048], P(None, 'narrow'), may hold values from -0.125 to 0.125
- w_key: bfloat16 [2048, 512], P(None, 'narrow'), may hold values from -0.125 to 0.125
- w_value: bfloat16 [2048, 512], P(None, 'narrow'), may hold values from -0.125 to 0.125
- w_out: bfloat16 [2048, 2048], P('narrow'), may hold values from -2 to 2
- ffn_gain: bfloat16 [2048], replicated, may hold values from 0.099609375 to 1.8984375
- w_gate: bfloat16 [2048, 8192], P(None, 'narrow'), may hold values from -0.125 to 0.125
- w_up: bfloat16 [2048, 8192], P(None, 'narrow'), may hold values from -0.125 to 0.125
- w_down: bfloat16 [8192, 2048], P('narrow'), may hold values from -0.0625 to 0.0625
- doc_lengths: int32 [12], replicated, may hold values from 1 to 2048, 4096 in all
- cotangent: bfloat16 [4096, 2048], P('wide'), may hold values from -6 to 6
Outputs:
- output: bfloat16 [4096, 2048], P('wide')
- input_grad: bfloat16 [4096, 2048], P('wide')
- grad_attn_gain: float32 [2048], P('wide')
- grad_query: float32 [2048, 2048], P('wide', 'narrow')
- grad_key: float32 [2048, 512], P('wide', 'narrow')
- grad_value: float32 [2048, 512], P('wide', 'narrow')
- grad_out: float32 [2048, 2048], P('narrow', 'wide')
- grad_ffn_gain: float32 [2048], P('wide')
- grad_gate: float32 [2048, 8192], P('wide', 'narrow')
- grad_up: float32 [2048, 8192], P('wide', 'narrow')
- grad_down: float32 [8192, 2048], P('narrow', 'wide')
Inputs may be any that keep to these rules, and one draw needn't show every extreme that they name: `doc_lengths`: the last entry is the padding at the row's end; the longest entry is exactly 2048.
All inputs are finite; a program needn't handle non-finite values.
Results may differ from a plain program's by a relative error of at most 0.02.
Values may be sent and summed in bfloat16 or wider, within the bound.
No kernel may reach another device: no remote copies, remote signals or barrier semaphores. Data moves between devices by JAX's collectives and lax.ppermute only.
A program may use at most 320 MiB of HBM per device.

v0:
```python
import math
import jax
import jax.numpy as jnp
import numpy as np
from jax import lax
from jax.sharding import PartitionSpec as P

HD = 64
QBLK = 512
DOCS = 12
NORM_EPS = 1e-05
MASKED_SCORE = -1e30


def inverse_frequencies(head_size):
    frequency = 1.0 / 500000.0 ** (np.arange(0, head_size, 2) / head_size)
    wavelength = 2 * math.pi / frequency
    smoothing = (8192.0 / wavelength - 1.0) / 3.0
    scaled_freq = np.where(wavelength > 8192.0, frequency / 32.0, frequency)
    middle_band = (wavelength <= 8192.0) & (wavelength >= 2048.0)
    scaled_freq = np.where(
        middle_band, (1 - smoothing) * frequency / 32.0 + smoothing * frequency, scaled_freq
    )
    return scaled_freq.astype(np.float32)


def doc_layout(doc_lengths, index):
    ends = jnp.cumsum(doc_lengths)
    passed = (index[:, None] >= ends[None, :]).astype(jnp.int32)
    segment = jnp.sum(passed, axis=1)
    offset = jnp.sum(passed * doc_lengths[None, :], axis=1)
    position = index - offset
    valid = index < ends[DOCS - 2]
    return (segment, position, valid)


def rotate(values, position, heads, direction):
    angle = position.astype(jnp.float32)[:, None] * jnp.asarray(inverse_frequencies(HD))[None, :]
    cosine = jnp.cos(angle)[:, None, :]
    sine = direction * jnp.sin(angle)[:, None, :]
    shaped = values.reshape(values.shape[0], heads, 2, HD // 2)
    first = shaped[:, :, 0]
    second = shaped[:, :, 1]
    return jnp.stack(
        [first * cosine - second * sine, second * cosine + first * sine], axis=2
    ).reshape(values.shape)


def contract_rows(left, right):
    return lax.dot_general(
        left, right, (((0,), (0,)), ((), ())), preferred_element_type=jnp.float32
    )


def contract_cols(left, right):
    return lax.dot_general(
        left, right, (((1,), (1,)), ((), ())), preferred_element_type=jnp.float32
    )


def head_scores(query_head, key_head, allowed):
    raw_scores = contract_cols(query_head, key_head)
    return jnp.where(allowed, raw_scores / math.sqrt(HD), MASKED_SCORE)


def norm_back(grad_normed, gain, values, inverse):
    scaled = grad_normed * gain
    return inverse * scaled - values * inverse**3 * jnp.mean(
        scaled * values, axis=-1, keepdims=True
    )


def body(
    tokens,
    attn_gain,
    w_query,
    w_key,
    w_value,
    w_out,
    ffn_gain,
    w_gate,
    w_up,
    w_down,
    doc_lengths,
    cotangent,
):
    rows = tokens.shape[0]
    total = rows * lax.axis_size("wide")
    heads = w_query.shape[1] // HD
    kv_heads = w_key.shape[1] // HD
    group = heads // kv_heads
    blocks = rows // QBLK
    local_index = lax.axis_index("wide") * rows + jnp.arange(rows, dtype=jnp.int32)
    segment, position, valid = doc_layout(doc_lengths, local_index)
    key_index = jnp.arange(total, dtype=jnp.int32)
    key_layout = doc_layout(doc_lengths, key_index)
    key_segment = key_layout[0]
    inputs = tokens.astype(jnp.float32)
    gain_one = attn_gain.astype(jnp.float32)
    gain_two = ffn_gain.astype(jnp.float32)
    inv_one = lax.rsqrt(jnp.mean(inputs * inputs, axis=-1, keepdims=True) + NORM_EPS)
    normed = (inputs * inv_one * gain_one).astype(jnp.bfloat16)
    query = jnp.dot(normed, w_query, preferred_element_type=jnp.float32)
    keys = jnp.dot(normed, w_key, preferred_element_type=jnp.float32)
    values = jnp.dot(normed, w_value, preferred_element_type=jnp.float32).astype(jnp.bfloat16)
    query_r = rotate(query, position, heads, 1.0).astype(jnp.bfloat16)
    keys_r = rotate(keys, position, kv_heads, 1.0).astype(jnp.bfloat16)
    packed = jnp.concatenate([keys_r, values], axis=1)
    gathered = lax.all_gather(packed, "wide", axis=0, tiled=True)
    width = kv_heads * HD
    all_keys = gathered[:, :width]
    all_values = gathered[:, width:]

    def block_mask(segment_block, index_block):
        return (segment_block[:, None] == key_segment[None, :]) & (
            index_block[:, None] >= key_index[None, :]
        )

    def attend(block_in):
        query_block, segment_block, index_block = block_in
        allowed = block_mask(segment_block, index_block)
        outputs = []
        totals = []
        for head in range(heads):
            column = head // group * HD
            scores = head_scores(
                query_block[:, head * HD : (head + 1) * HD],
                all_keys[:, column : column + HD],
                allowed,
            )
            row_max = jnp.max(scores, axis=1, keepdims=True)
            exponent = jnp.exp(scores - row_max)
            row_sum = jnp.sum(exponent, axis=1, keepdims=True)
            probs = (exponent / row_sum).astype(jnp.bfloat16)
            outputs.append(
                jnp.dot(
                    probs, all_values[:, column : column + HD], preferred_element_type=jnp.float32
                )
            )
            totals.append(row_max[:, 0] + jnp.log(row_sum[:, 0]))
        return (jnp.concatenate(outputs, axis=1), jnp.stack(totals, axis=1))

    query_blocks = query_r.reshape(blocks, QBLK, heads * HD)
    segment_blocks = segment.reshape(blocks, QBLK)
    index_blocks = local_index.reshape(blocks, QBLK)
    attended, log_sums = lax.map(attend, (query_blocks, segment_blocks, index_blocks))
    valid_rows = valid[:, None]
    mixed = jnp.where(valid_rows, attended.reshape(rows, heads * HD), 0.0).astype(jnp.bfloat16)
    attn_part = jnp.dot(mixed, w_out, preferred_element_type=jnp.float32)
    hidden_one = inputs + lax.psum(attn_part, "narrow")
    inv_two = lax.rsqrt(jnp.mean(hidden_one * hidden_one, axis=-1, keepdims=True) + NORM_EPS)
    normed_two = (hidden_one * inv_two * gain_two).astype(jnp.bfloat16)
    gate = jnp.dot(normed_two, w_gate, preferred_element_type=jnp.float32)
    up_proj = jnp.dot(normed_two, w_up, preferred_element_type=jnp.float32)
    sigmoid_gate = jax.nn.sigmoid(gate)
    silu_gate = gate * sigmoid_gate
    activ = (silu_gate * up_proj).astype(jnp.bfloat16)
    ffn_part = jnp.dot(activ, w_down, preferred_element_type=jnp.float32)
    grad_down = contract_rows(activ, cotangent)
    d_activ = contract_cols(cotangent, w_down)
    d_gate = (d_activ * up_proj * sigmoid_gate * (1.0 + gate * (1.0 - sigmoid_gate))).astype(
        jnp.bfloat16
    )
    d_up = (d_activ * silu_gate).astype(jnp.bfloat16)
    grad_gate = contract_rows(normed_two, d_gate)
    grad_up = contract_rows(normed_two, d_up)
    norm_two_part = contract_cols(d_gate, w_gate) + contract_cols(d_up, w_up)
    output = (
        hidden_one + lax.psum(ffn_part.astype(jnp.bfloat16), "narrow").astype(jnp.float32)
    ).astype(jnp.bfloat16)
    d_norm_two = lax.psum(norm_two_part.astype(jnp.bfloat16), "narrow").astype(jnp.float32)
    grad_ffn_gain = jnp.sum(d_norm_two * hidden_one * inv_two, axis=0)
    d_hidden = cotangent.astype(jnp.float32) + norm_back(d_norm_two, gain_two, hidden_one, inv_two)
    d_hidden_b = d_hidden.astype(jnp.bfloat16)
    grad_out = contract_rows(mixed, d_hidden_b)
    d_mixed = jnp.where(
        valid_rows,
        contract_cols(d_hidden_b, w_out).astype(jnp.bfloat16),
        jnp.zeros((), jnp.bfloat16),
    )

    def attend_back(carry, block_in):
        query_block, grad_block, lse_block, segment_block, index_block = block_in
        allowed = block_mask(segment_block, index_block)
        query_grads = []
        key_terms = [None] * kv_heads
        value_terms = [None] * kv_heads
        for head in range(heads):
            kv_index = head // group
            column = kv_index * HD
            query_head = query_block[:, head * HD : (head + 1) * HD]
            grad_head = grad_block[:, head * HD : (head + 1) * HD]
            key_head = all_keys[:, column : column + HD]
            value_head = all_values[:, column : column + HD]
            scores = head_scores(query_head, key_head, allowed)
            probs = jnp.where(allowed, jnp.exp(scores - lse_block[:, head : head + 1]), 0.0)
            prob_grad = contract_cols(grad_head, value_head)
            delta = jnp.sum(probs * prob_grad, axis=1, keepdims=True)
            d_scores = (probs * (prob_grad - delta)).astype(jnp.bfloat16)
            query_grads.append(
                jnp.dot(d_scores, key_head, preferred_element_type=jnp.float32) / math.sqrt(HD)
            )
            key_term = contract_rows(d_scores, query_head) / math.sqrt(HD)
            value_term = contract_rows(probs.astype(jnp.bfloat16), grad_head)
            if key_terms[kv_index] is None:
                key_terms[kv_index] = key_term
                value_terms[kv_index] = value_term
            else:
                key_terms[kv_index] = key_terms[kv_index] + key_term
                value_terms[kv_index] = value_terms[kv_index] + value_term
        update = jnp.concatenate(key_terms + value_terms, axis=1)
        return (carry + update, jnp.concatenate(query_grads, axis=1))

    start_terms = jnp.zeros((total, 2 * width), jnp.float32)
    grad_blocks = d_mixed.reshape(blocks, QBLK, heads * HD)
    kv_terms, query_grad_blocks = lax.scan(
        attend_back,
        start_terms,
        (query_blocks, grad_blocks, log_sums, segment_blocks, index_blocks),
    )
    d_kv = lax.psum_scatter(
        kv_terms.astype(jnp.bfloat16), "wide", scatter_dimension=0, tiled=True
    ).astype(jnp.float32)
    d_query = rotate(query_grad_blocks.reshape(rows, heads * HD), position, heads, -1.0).astype(
        jnp.bfloat16
    )
    d_keys = rotate(d_kv[:, :width], position, kv_heads, -1.0).astype(jnp.bfloat16)
    d_values = d_kv[:, width:].astype(jnp.bfloat16)
    grad_query = contract_rows(normed, d_query)
    grad_key = contract_rows(normed, d_keys)
    grad_value = contract_rows(normed, d_values)
    norm_one_part = (
        contract_cols(d_query, w_query)
        + contract_cols(d_keys, w_key)
        + contract_cols(d_values, w_value)
    )
    d_norm_one = lax.psum(norm_one_part.astype(jnp.bfloat16), "narrow").astype(jnp.float32)
    grad_attn_gain = jnp.sum(d_norm_one * inputs * inv_one, axis=0)
    input_grad = (d_hidden + norm_back(d_norm_one, gain_one, inputs, inv_one)).astype(jnp.bfloat16)
    summed = (
        lax.psum_scatter(
            grad_attn_gain.astype(jnp.bfloat16), "wide", scatter_dimension=0, tiled=True
        ).astype(jnp.float32),
        lax.psum_scatter(
            grad_query.astype(jnp.bfloat16), "wide", scatter_dimension=0, tiled=True
        ).astype(jnp.float32),
        lax.psum_scatter(
            grad_key.astype(jnp.bfloat16), "wide", scatter_dimension=0, tiled=True
        ).astype(jnp.float32),
        lax.psum_scatter(
            grad_value.astype(jnp.bfloat16), "wide", scatter_dimension=0, tiled=True
        ).astype(jnp.float32),
        lax.psum_scatter(
            grad_out.astype(jnp.bfloat16), "wide", scatter_dimension=1, tiled=True
        ).astype(jnp.float32),
        lax.psum_scatter(
            grad_ffn_gain.astype(jnp.bfloat16), "wide", scatter_dimension=0, tiled=True
        ).astype(jnp.float32),
        lax.psum_scatter(
            grad_gate.astype(jnp.bfloat16), "wide", scatter_dimension=0, tiled=True
        ).astype(jnp.float32),
        lax.psum_scatter(
            grad_up.astype(jnp.bfloat16), "wide", scatter_dimension=0, tiled=True
        ).astype(jnp.float32),
        lax.psum_scatter(
            grad_down.astype(jnp.bfloat16), "wide", scatter_dimension=1, tiled=True
        ).astype(jnp.float32),
    )
    gain_attn = summed[0]
    gain_ffn = summed[5]
    return (
        output,
        input_grad,
        gain_attn,
        summed[1],
        summed[2],
        summed[3],
        summed[4],
        gain_ffn,
        summed[6],
        summed[7],
        summed[8],
    )


def solution(mesh):
    in_specs = (
        P("wide", None),
        P(),
        P(None, "narrow"),
        P(None, "narrow"),
        P(None, "narrow"),
        P("narrow", None),
        P(),
        P(None, "narrow"),
        P(None, "narrow"),
        P("narrow", None),
        P(),
        P("wide", None),
    )
    out_specs = (
        P("wide", None),
        P("wide", None),
        P("wide"),
        P("wide", "narrow"),
        P("wide", "narrow"),
        P("wide", "narrow"),
        P("narrow", "wide"),
        P("wide"),
        P("wide", "narrow"),
        P("wide", "narrow"),
        P("narrow", "wide"),
    )
    return jax.shard_map(body, mesh=mesh, in_specs=in_specs, out_specs=out_specs, check_vma=False)
```

profile of v0, /device:TPU:0, one launch (start us, length us, event | category | flops | bytes accessed | tf_op | source)
XLA Modules:
  0.0 1095.4 jit_solution(12022537940424208202)
XLA Ops:
  12.5 2.6 convolution_convert_fusion.9
  19.5 3.6 fusion.159
  24.1 25.7 %all-gather.2.cloned.1.call-done = bf16[4096,256]{0,1:T(8,128)(2,1)} async-done(((bf16[512,256]{0,1:T(8,128)(2,1)}), bf16[4096,256]{0,1:T(8,128)(2,1)}) %all-gather.2.cloned.1.call-update) | async-done | bytes 2097168 | tf_op jit(solution)/shard_map/all_gather | solution.py:109
  49.8 3.6 fusion.176
  53.4 3.2 copy-done.7
  57.9 3.6 fusion.175
  62.9 4.1 fusion.174
  70.2 3.6 fusion.173
  77.1 3.6 fusion.172
  80.7 3.3 copy-done.10
  85.3 3.6 fusion.171
  90.2 4.5 fusion.170
  96.0 7.2 fusion.169
  103.1 4.8 fusion.1
  107.9 5.0 fusion.60
  116.7 5.4 fusion.57
  131.1 3.3 fusion.71
  134.7 103.2 %all-reduce.8.cloned.1.call-done = f32[512,2048]{1,0:T(8,128)} async-done(((f32[512,2048]{1,0:T(8,128)}), f32[512,2048]{1,0:T(8,128)}) %all-reduce.8.cloned.1.call-update) | async-done | bytes 4194320 | tf_op jit(solution)/shard_map/psum | solution.py:150
  237.9 3.5 multiply_reduce_fusion.8
  241.9 9.3 fusion.178
  251.2 6.3 fusion.177
  257.5 12.0 %multiply_convert_fusion.8 = (bf16[512,2048]{1,0:T(8,128)(2,1)}, bf16[512,2048]{1,0:T(8,128)(2,1)}, bf16[512,2048]{1,0:T(8,128)(2,1)}) fusion(f32[512,2048]{1,0:T(8,128)} %fusion.177, f32[512,2048]{1,0:T(8,128)S(1)} %fusion.178, bf16[512,2048]{1,0:T(8,128)(2,1)S(1)} %copy-done.36, bf16[2048,2048]{1,0:T(8,128)(2,1)} %param.25), kind=kOutput, calls=%fused_computation.118 | convolution fusion | flops 4310695936 | bytes 25165824 | tf_op jit(solution)/shard_map/dot_general | solution.py:56
  269.5 7.8 fusion.179
  277.3 9.4 add_convert_fusion.1
  287.2 69.3 %all-reduce.10.cloned.1.call-done = bf16[512,2048]{1,0:T(8,128)(2,1)} async-done(((bf16[512,2048]{1,0:T(8,128)(2,1)}), bf16[512,2048]{1,0:T(8,128)(2,1)}) %all-reduce.10.cloned.1.call-update) | async-done | bytes 2097168 | tf_op jit(solution)/shard_map/psum | solution.py:171
  356.5 4.9 fusion.25
  361.4 3.6 fusion.22
  376.2 2.6 convolution_add_fusion.4
  378.9 3.3 fusion.16
  387.2 3.3 fusion.17
  390.5 4.6 fusion.78
  395.0 4.6 fusion.80
  399.6 4.9 fusion.94
  405.8 4.6 fusion.98
  410.4 4.5 fusion.100
  415.0 26.5 %multiply_reduce_fusion = (f32[512]{0:T(512)S(1)}, f32[512]{0:T(512)S(1)}, f32[512]{0:T(512)S(1)}, f32[512]{0:T(512)S(1)}, f32[512]{0:T(512)S(1)}, /*index=5*/f32[512,4096]{1,0:T(8,128)}) fusion(f32[512,4096]{1,0:T(8,128)} %copy-done.7, f32[512]{0:T(512)S(1)} %log_add_fusion, s32[512]{0:T(512)S(1)} %iota_add_fusion, s32[4096]{0:T(1024)S(1)} %convert_reduce_fusion, ...), kind=kOutput, calls=%fused_computation.7 | convolution fusion | flops 316667392 | bytes 84516864 | tf_op jit(solution)/shard_map/while/body/eval_jaxpr/dot_general | solution.py:56
  441.5 25.5 %multiply_reduce_fusion.1 = (f32[512]{0:T(512)S(1)}, f32[512]{0:T(512)S(1)}, f32[512]{0:T(512)S(1)}, bf16[512,4096]{1,0:T(8,128)(2,1)}, f32[512,4096]{1,0:T(8,128)}) fusion(f32[512,4096]{1,0:T(8,128)} %copy-done.4, f32[512]{0:T(512)S(1)} %get-tuple-element.145, s32[512]{0:T(512)S(1)} %iota_add_fusion, s32[4096]{0:T(1024)S(1)} %convert_reduce_fusion, ...), kind=kOutput, calls=%fused_computation.10 | convolution fusion | flops 310376960 | bytes 71929856 | tf_op jit(solution)/shard_map/while/body/eval_jaxpr/dot_general | solution.py:56
  467.0 21.2 %multiply_convert_fusion.2 = (bf16[512,4096]{1,0:T(8,128)(2,1)}, bf16[512,4096]{1,0:T(8,128)(2,1)}, bf16[512,4096]{1,0:T(8,128)(2,1)S(1)}) fusion(f32[512,4096]{1,0:T(8,128)} %fusion.78, f32[512]{0:T(512)S(1)} %get-tuple-element.88, f32[512,4096]{1,0:T(8,128)} %copy-done.8, f32[512]{0:T(512)S(1)} %get-tuple-element.146, s32[512]{0:T(512)S(1)} %iota_add_fusion, ...), kind=kLoop, calls=%fused_computation.12 | loop fusion | flops 37748736 | bytes 62947328 | tf_op jit(solution)/shard_map/while/body/eval_jaxpr/convert_element_type | solution.py:199
  492.1 27.0 %multiply_convert_fusion.1 = (bf16[512,4096]{1,0:T(8,128)(2,1)}, bf16[512,4096]{1,0:T(8,128)(2,1)}, bf16[512,4096]{1,0:T(8,128)(2,1)}, bf16[512,4096]{1,0:T(8,128)(2,1)}) fusion(f32[512,4096]{1,0:T(8,128)} %get-tuple-element.140, f32[512]{0:T(512)S(1)} %get-tuple-element.74, f32[512,4096]{1,0:T(8,128)} %copy-done.4, f32[512]{0:T(512)S(1)} %get-tuple-element.145, ...), kind=kLoop, calls=%fused_computation.9 | loop fusion | flops 48234496 | bytes 83922944 | tf_op jit(solution)/shard_map/while/body/eval_jaxpr/convert_element_type | solution.py:199
  519.2 3.2 fusion.145
  533.6 4.7 convolution_convert_fusion.3
  538.4 3.9 fusion.68
  542.4 3.7 fusion.67
  555.0 2.9 convolution_convert_fusion.4
  558.0 11.5 %reduce-scatter.9.cloned.1.call-done = bf16[512,256]{0,1:T(8,128)(2,1)} async-done(((bf16[4096,256]{0,1:T(8,128)(2,1)}), bf16[512,256]{0,1:T(8,128)(2,1)}) %reduce-scatter.9.cloned.1.call-update) | async-done | bytes 262160 | tf_op jit(solution)/shard_map/reduce_scatter | solution.py:221
  572.8 10.0 convolution_convert_fusion.5
  584.8 3.0 fusion.180
  591.0 10.1 convolution_convert_fusion.1
  601.3 10.1 convolution_convert_fusion.2
  611.4 10.3 convolution_convert_fusion
  625.4 17.5 %reduce-scatter.11.cloned.1.call-done = bf16[256,512]{1,0:T(8,128)(2,1)} async-done(((bf16[2048,512]{1,0:T(8,128)(2,1)}), bf16[256,512]{1,0:T(8,128)(2,1)}) %reduce-scatter.11.cloned.1.call-update) | async-done | bytes 262160 | tf_op jit(solution)/shard_map/reduce_scatter | solution.py:244
  644.7 30.1 %reduce-scatter.13.cloned.1.call-done = bf16[256,128]{1,0:T(8,128)(2,1)} async-done(((bf16[2048,128]{1,0:T(8,128)(2,1)}), bf16[256,128]{1,0:T(8,128)(2,1)}) %reduce-scatter.13.cloned.1.call-update) | async-done | bytes 65552 | tf_op jit(solution)/shard_map/reduce_scatter | solution.py:247
  676.2 30.1 %reduce-scatter.15.cloned.1.call-done = bf16[256,128]{1,0:T(8,128)(2,1)} async-done(((bf16[2048,128]{1,0:T(8,128)(2,1)}), bf16[256,128]{1,0:T(8,128)(2,1)}) %reduce-scatter.15.cloned.1.call-update) | async-done | bytes 65552 | tf_op jit(solution)/shard_map/reduce_scatter | solution.py:250
  707.8 105.0 %all-reduce.12.cloned.1.call-done = (bf16[512,2048]{1,0:T(8,128)(2,1)}, bf16[512,2048]{1,0:T(8,128)(2,1)}) async-done(((bf16[512,2048]{1,0:T(8,128)(2,1)}, bf16[512,2048]{1,0:T(8,128)(2,1)}), (bf16[512,2048]{1,0:T(8,128)(2,1)}, bf16[512,2048]{1,0:T(8,128)(2,1)})) %all-reduce.12.cloned.1.call-update) | async-done | bytes 4194320 | tf_op jit(solution)/shard_map/psum | solution.py:169
  812.8 3.2 fusion.32
  816.0 17.4 %all-reduce.2 = (bf16[2048]{0:T(1024)(128)(2,1)S(1)}, bf16[2048]{0:T(1024)(128)(2,1)S(1)}) all-reduce(bf16[2048]{0:T(1024)(128)(2,1)S(1)} %get-tuple-element.67, bf16[2048]{0:T(1024)(128)(2,1)S(1)} %copy-done.52), channel_id=3, replica_groups=mesh['wide'=8,'narrow'=4] {'wide'}, use_global_device_ids=true, to_apply=%region_38.39.clone | all-reduce | flops 4096 | bytes 16384
  834.7 5.1 add_convert_fusion.2
  840.9 2.6 fusion.20
  843.5 61.7 %reduce-scatter.21.cloned.1.call-done = bf16[256,2048]{1,0:T(8,128)(2,1)} async-done(((bf16[2048,2048]{1,0:T(8,128)(2,1)}), bf16[256,2048]{1,0:T(8,128)(2,1)}) %reduce-scatter.21.cloned.1.call-update) | async-done | bytes 1048592 | tf_op jit(solution)/shard_map/reduce_scatter | solution.py:262
  905.2 2.8 convert_element_type.315
  908.0 87.4 %reduce-scatter.19.cloned.1.call-done = bf16[256,2048]{1,0:T(8,128)(2,1)} async-done(((bf16[2048,2048]{1,0:T(8,128)(2,1)}), bf16[256,2048]{1,0:T(8,128)(2,1)}) %reduce-scatter.19.cloned.1.call-update) | async-done | bytes 1048592 | tf_op jit(solution)/shard_map/reduce_scatter | solution.py:259
  995.4 2.8 convert_element_type.313
  998.2 87.4 %reduce-scatter.23.cloned.1.call-done = bf16[2048,256]{1,0:T(8,128)(2,1)} async-done(((bf16[2048,2048]{1,0:T(8,128)(2,1)}), bf16[2048,256]{1,0:T(8,128)(2,1)}) %reduce-scatter.23.cloned.1.call-update) | async-done | bytes 1048592 | tf_op jit(solution)/shard_map/reduce_scatter | solution.py:265
  1085.7 2.7 convert_element_type.317
  (281 shorter events, 97.3 us)
Async XLA Ops:
  7.2 123.9 %copy-start = (bf16[512,2048]{1,0:T(8,128)(2,1)S(1)}, bf16[512,2048]{1,0:T(8,128)(2,1)}, u32[]{:S(2)}) copy-start(bf16[512,2048]{1,0:T(8,128)(2,1)} %param.21) | copy-start | bytes 6291460
  7.2 7.9 copy-start.40
  7.2 42.6 %all-gather.2.cloned.1.call-start = ((), (), s32[]{:S(2)}) async-start(), calls=%async_computation.8 | async-start | bytes 2359296 | tf_op jit(solution)/shard_map/all_gather | solution.py:109
  10.1 9.4 copy-start.50
  10.9 4.2 copy-start.26
  12.5 6.9 copy-start.48
  12.5 3.6 copy-start.57
  17.0 6.0 copy-start.37
  17.9 220.0 %all-reduce.8.cloned.1.call-start = ((), (), s32[]{:S(2)}) async-start(), calls=%async_computation.9 | async-start | bytes 8388608 | tf_op jit(solution)/shard_map/psum | solution.py:150
  19.3 345.7 %copy-start.53 = (pred[512]{0:T(512)(128)(4,1)}, pred[512]{0:T(512)(128)(4,1)S(1)}, u32[]{:S(2)}) copy-start(pred[512]{0:T(512)(128)(4,1)S(1)} %fusion.150) | copy-start | bytes 1540
  61.6 64.6 %copy-start.4 = (f32[512,4096]{1,0:T(8,128)}, f32[512,4096]{1,0:T(8,128)S(1)}, u32[]{:S(2)}) copy-start(f32[512,4096]{1,0:T(8,128)S(1)} %get-tuple-element.136) | copy-start | bytes 25165828
  66.9 3.3 copy-start.8
  88.9 25.9 %copy-start.5 = (f32[512,4096]{1,0:T(8,128)}, f32[512,4096]{1,0:T(8,128)S(1)}, u32[]{:S(2)}) copy-start(f32[512,4096]{1,0:T(8,128)S(1)} %get-tuple-element.128) | copy-start | bytes 25165828
  94.7 18.3 %copy-start.6 = (f32[512,4096]{1,0:T(8,128)}, f32[512,4096]{1,0:T(8,128)S(1)}, u32[]{:S(2)}) copy-start(f32[512,4096]{1,0:T(8,128)S(1)} %get-tuple-element.126) | copy-start | bytes 25165828
  103.1 4.8 copy-start.24
  114.8 7.2 slice-start.16
  116.6 5.4 slice-start.17
  116.7 7.2 slice-start.10
  124.4 3.7 slice-start.6
  131.1 3.6 copy-start.56
  134.4 222.1 %all-reduce.10.cloned.1.call-start = ((), (), s32[]{:S(2)}) async-start(), calls=%async_computation.10 | async-start | bytes 4194304 | tf_op jit(solution)/shard_map/psum | solution.py:171
  241.4 9.8 copy-start.2
  241.4 9.8 slice-start.22
  241.8 9.4 copy-start.35
  241.8 9.4 slice-start.23
  251.2 6.3 copy-start.36
  269.5 7.8 copy-start.59
  286.7 282.8 %reduce-scatter.9.cloned.1.call-start = ((), (), s32[]{:S(2)}) async-start(), calls=%async_computation.11 | async-start | bytes 2359296 | tf_op jit(solution)/shard_map/reduce_scatter | solution.py:221
  356.5 4.9 copy-start.3
  356.5 10.7 slice-start.14
  361.4 5.8 slice-start.15
  365.1 4.6 slice-start.18
  367.2 5.4 slice-start.4
  370.2 4.9 slice-start.2
  370.2 8.7 slice-start.20
  372.7 3.6 slice-start.3
  372.7 6.2 slice-start.21
  376.2 6.0 slice-start.12
  376.2 8.4 slice-start
  378.9 3.3 slice-start.13
  378.9 5.8 slice-start.1
  382.2 4.9 slice-start.8
  387.2 3.3 copy-start.25
  467.0 23.3 %copy-start.34 = (bf16[512,8,2,32]{0,3,2,1:T(8,128)(2,1)S(1)}, bf16[512,8,2,32]{0,3,2,1:T(8,128)(2,1)}, u32[]{:S(2)}) copy-start(bf16[512,8,2,32]{0,3,2,1:T(8,128)(2,1)} %pad_maximum_fusion.1) | copy-start | bytes 1572868
  519.1 3.5 copy-start.13
  519.1 3.7 copy-start.33
  533.5 90.1 %reduce-scatter.17.cloned.1.call-start = ((), (), s32[]{:S(2)}) async-start(), calls=%async_computation.15 | async-start | bytes 2359296 | tf_op jit(solution)/shard_map/reduce_scatter | solution.py:253
  538.4 104.5 %reduce-scatter.11.cloned.1.call-start = ((), (), s32[]{:S(2)}) async-start(), calls=%async_computation.12 | async-start | bytes 2359296 | tf_op jit(solution)/shard_map/reduce_scatter | solution.py:244
  538.4 7.7 copy-start.22
  542.3 5.2 copy-start.18
  555.0 15.5 %copy-start.28 = (bf16[512,2048]{1,0:T(8,128)(2,1)S(1)}, bf16[512,2048]{1,0:T(8,128)(2,1)}, u32[]{:S(2)}) copy-start(bf16[512,2048]{1,0:T(8,128)(2,1)} %param.16) | copy-start | bytes 6291460
  557.9 116.8 %reduce-scatter.13.cloned.1.call-start = ((), (), s32[]{:S(2)}) async-start(), calls=%async_computation.13 | async-start | bytes 589824 | tf_op jit(solution)/shard_map/reduce_scatter | solution.py:247
  572.4 133.9 %reduce-scatter.15.cloned.1.call-start = ((), (), s32[]{:S(2)}) async-start(), calls=%async_computation.14 | async-start | bytes 589824 | tf_op jit(solution)/shard_map/reduce_scatter | solution.py:250
  572.8 10.1 copy-start.47
  584.7 228.1 %all-reduce.12.cloned.1.call-start = ((), (), s32[]{:S(2)}) async-start(), calls=%async_computation.19 | async-start | bytes 8388608 | tf_op jit(solution)/shard_map/psum | solution.py:169
  590.9 314.3 %reduce-scatter.21.cloned.1.call-start = ((), (), s32[]{:S(2)}) async-start(), calls=%async_computation.17 | async-start | bytes 9437184 | tf_op jit(solution)/shard_map/reduce_scatter | solution.py:262
  601.1 394.3 %reduce-scatter.19.cloned.1.call-start = ((), (), s32[]{:S(2)}) async-start(), calls=%async_computation.16 | async-start | bytes 9437184 | tf_op jit(solution)/shard_map/reduce_scatter | solution.py:259
  611.4 474.3 %reduce-scatter.23.cloned.1.call-start = ((), (), s32[]{:S(2)}) async-start(), calls=%async_computation.18 | async-start | bytes 9437184 | tf_op jit(solution)/shard_map/reduce_scatter | solution.py:265
  621.7 194.2 %copy-start.52 = (bf16[2048]{0:T(1024)(128)(2,1)S(1)}, bf16[2048]{0:T(1024)(128)(2,1)}, u32[]{:S(2)}) copy-start(bf16[2048]{0:T(1024)(128)(2,1)} %get-tuple-element.65) | copy-start | bytes 12292
  642.9 196.9 %copy-start.55 = (f32[512]{0:T(512)S(1)}, f32[512]{0:T(512)}, u32[]{:S(2)}) copy-start(f32[512]{0:T(512)} %get-tuple-element.119) | copy-start | bytes 6148
  834.7 5.1 copy-start.29
  834.7 5.1 copy-start.31
  834.7 6.2 copy-start.32
  840.9 247.5 %copy-start.1 = (bf16[512,2048]{1,0:T(8,128)(2,1)S(1)}, bf16[512,2048]{1,0:T(8,128)(2,1)}, u32[]{:S(2)}) copy-start(bf16[512,2048]{1,0:T(8,128)(2,1)} %param.21) | copy-start | bytes 6291460
  (32 other events, 72.7 us)
Sparse Core Ops, SparseCore 0:
  18.0 31.7 all-gather.1
  134.5 103.3 all-reduce.7
  286.8 69.6 all-reduce.9
  533.6 35.8 reduce-scatter.8
  571.6 34.4 reduce-scatter.16
  608.3 34.5 reduce-scatter.10
  645.1 29.5 reduce-scatter.12
  677.1 29.1 reduce-scatter.14
  710.4 102.3 all-reduce.11
  815.0 90.1 reduce-scatter.20
  907.6 87.7 reduce-scatter.18
  997.7 87.9 reduce-scatter.22
where the time goes:
time: 1100 us
  waiting for transfers between devices  629 us (57%)
  matrix products  293 us (27%)
  other arithmetic  112 us (10%)
  local copies, waits for them, and re-layouts  25.3 us (2%)
  blocking collectives  17.4 us (2%)
  between operations  16.3 us (1%)
    dot_general x23, matrix products, contract_cols(): lax.dot_general(left, right, (((1,), (1,)), ((), ())), preferred_element_...  147 us
    psum x1, waiting for transfers between devices, body(): lax.psum(ffn_part.astype(jnp.bfloat16), 'narrow').astype(jnp.float32)  105 us
    psum x1, waiting for transfers between devices, body(): hidden_one = inputs + lax.psum(attn_part, 'narrow')  103 us
    reduce_scatter x1, waiting for transfers between devices, body(): lax.psum_scatter(grad_down.astype(jnp.bfloat16), 'wide', scatter_dimensio...  87.4 us
    reduce_scatter x1, waiting for transfers between devices, body(): lax.psum_scatter(grad_gate.astype(jnp.bfloat16), 'wide', scatter_dimensio...  87.4 us
    dot_general x23, matrix products, contract_rows(): lax.dot_general(left, right, (((0,), (0,)), ((), ())), preferred_element_...  73.2 us
    psum x1, waiting for transfers between devices, body(): lax.psum(norm_two_part.astype(jnp.bfloat16), 'narrow').astype(jnp.float32)  69.3 us
    reduce_scatter x1, waiting for transfers between devices, body(): lax.psum_scatter(grad_up.astype(jnp.bfloat16), 'wide', scatter_dimension=...  61.7 us
  transfers between devices with their start and end apart: 12, of which 11 were waited for; matrix products, arithmetic and copies ran while one was open for 10% of the time, Pallas kernels for 0%

commit v1 on v0

--- a/solution.py
+++ b/solution.py
@@ -147,7 +147,7 @@
     valid_rows = valid[:, None]
     mixed = jnp.where(valid_rows, attended.reshape(rows, heads * HD), 0.0).astype(jnp.bfloat16)
     attn_part = jnp.dot(mixed, w_out, preferred_element_type=jnp.float32)
-    hidden_one = inputs + lax.psum(attn_part, "narrow")
+    hidden_one = inputs + jnp.sum(lax.all_gather(attn_part, "narrow"), axis=0)
     inv_two = lax.rsqrt(jnp.mean(hidden_one * hidden_one, axis=-1, keepdims=True) + NORM_EPS)
     normed_two = (hidden_one * inv_two * gain_two).astype(jnp.bfloat16)
     gate = jnp.dot(normed_two, w_gate, preferred_element_type=jnp.float32)

time: 1100 us -> 1160 us (1.055)
  waiting for transfers between devices: 629 us -> 683 us
    all_gather x0 -> x1, waiting for transfers between devices: none -> 157 us  [body(): hidden_one = inputs + jnp.sum(lax.all_gather(attn_part, 'narrow'), axis=0)]
    psum x1 -> x0, waiting for transfers between devices: 103 us -> none  [body(): hidden_one = inputs + lax.psum(attn_part, 'narrow')]
  transfers between devices with their start and end apart: 12 -> 12, of which waited for: 11 -> 11; matrix products, arithmetic and copies ran while one was open for 10% -> 9% of each run, Pallas kernels for 0% -> 0%
where the time goes in v1:
time: 1160 us
  waiting for transfers between devices  683 us (59%)
  matrix products  294 us (25%)
  other arithmetic  122 us (11%)
  local copies, waits for them, and re-layouts  25.4 us (2%)
  blocking collectives  17.4 us (1%)
  between operations  16.3 us (1%)
    all_gather x1, waiting for transfers between devices, body(): hidden_one = inputs + jnp.sum(lax.all_gather(attn_part, 'narrow'), axis=0)  157 us
    dot_general x23, matrix products, contract_cols(): lax.dot_general(left, right, (((1,), (1,)), ((), ())), preferred_element_...  147 us
    psum x1, waiting for transfers between devices, body(): lax.psum(ffn_part.astype(jnp.bfloat16), 'narrow').astype(jnp.float32)  105 us
    reduce_scatter x1, waiting for transfers between devices, body(): lax.psum_scatter(grad_gate.astype(jnp.bfloat16), 'wide', scatter_dimensio...  87.4 us
    reduce_scatter x1, waiting for transfers between devices, body(): lax.psum_scatter(grad_down.astype(jnp.bfloat16), 'wide', scatter_dimensio...  87.3 us
    dot_general x23, matrix products, contract_rows(): lax.dot_general(left, right, (((0,), (0,)), ((), ())), preferred_element_...  73.2 us
    psum x1, waiting for transfers between devices, body(): lax.psum(norm_two_part.astype(jnp.bfloat16), 'narrow').astype(jnp.float32)  69.3 us
    reduce_scatter x1, waiting for transfers between devices, body(): lax.psum_scatter(grad_up.astype(jnp.bfloat16), 'wide', scatter_dimension=...  61.6 us
  transfers between devices with their start and end apart: 12, of which 11 were waited for; matrix products, arithmetic and copies ran while one was open for 9% of the time, Pallas kernels for 0%

profile of v1, /device:TPU:0, one launch (start us, length us, event | category | flops | bytes accessed | tf_op | source)
XLA Modules:
  0.0 1159.7 jit_solution(1520132969177941962)
XLA Ops:
  19.5 3.6 fusion.159
  24.1 25.7 %all-gather.4.cloned.1.call-done = bf16[4096,256]{0,1:T(8,128)(2,1)} async-done(((bf16[512,256]{0,1:T(8,128)(2,1)}), bf16[4096,256]{0,1:T(8,128)(2,1)}) %all-gather.4.cloned.1.call-update) | async-done | bytes 2097168 | tf_op jit(solution)/shard_map/all_gather | solution.py:109
  49.8 3.6 fusion.176
  53.4 3.3 copy-done.7
  58.0 3.6 fusion.175
  63.0 4.1 fusion.174
  70.3 3.6 fusion.173
  77.2 3.6 fusion.172
  80.8 3.3 copy-done.10
  85.3 3.6 fusion.171
  90.3 4.5 fusion.170
  96.1 7.1 fusion.169
  103.2 4.8 fusion.1
  108.0 5.0 fusion.60
  116.7 5.4 fusion.57
  131.2 3.3 fusion.71
  134.6 157.0 %all-gather.6.cloned.1.call-done = f32[2048,2048]{1,0:T(8,128)} async-done(((f32[512,2048]{1,0:T(8,128)}), f32[2048,2048]{1,0:T(8,128)}) %all-gather.6.cloned.1.call-update) | async-done | bytes 16777232 | tf_op jit(solution)/shard_map/all_gather | solution.py:150
  291.6 10.2 reduce_sum.262
  301.7 3.5 multiply_reduce_fusion.8
  305.7 9.6 fusion.178
  315.4 6.3 fusion.177
  321.6 12.0 %multiply_convert_fusion.8 = (bf16[512,2048]{1,0:T(8,128)(2,1)}, bf16[512,2048]{1,0:T(8,128)(2,1)}, bf16[512,2048]{1,0:T(8,128)(2,1)}) fusion(f32[512,2048]{1,0:T(8,128)} %fusion.177, f32[512,2048]{1,0:T(8,128)S(1)} %fusion.178, bf16[512,2048]{1,0:T(8,128)(2,1)S(1)} %copy-done.36, bf16[2048,2048]{1,0:T(8,128)(2,1)} %param.25), kind=kOutput, calls=%fused_computation.118 | convolution fusion | flops 4310695936 | bytes 25165824 | tf_op jit(solution)/shard_map/dot_general | solution.py:56
  333.6 7.8 fusion.179
  341.4 9.4 add_convert_fusion.1
  351.4 69.3 %all-reduce.7.cloned.1.call-done = bf16[512,2048]{1,0:T(8,128)(2,1)} async-done(((bf16[512,2048]{1,0:T(8,128)(2,1)}), bf16[512,2048]{1,0:T(8,128)(2,1)}) %all-reduce.7.cloned.1.call-update) | async-done | bytes 2097168 | tf_op jit(solution)/shard_map/psum | solution.py:171
  420.7 4.9 fusion.25
  425.6 3.6 fusion.22
  440.4 2.6 convolution_add_fusion.4
  443.1 3.3 fusion.16
  451.3 3.3 fusion.17
  454.6 4.6 fusion.78
  459.2 4.6 fusion.80
  463.8 4.9 fusion.94
  470.0 4.5 fusion.98
  474.5 4.6 fusion.100
  479.1 26.5 %multiply_reduce_fusion = (f32[512]{0:T(512)S(1)}, f32[512]{0:T(512)S(1)}, f32[512]{0:T(512)S(1)}, f32[512]{0:T(512)S(1)}, f32[512]{0:T(512)S(1)}, /*index=5*/f32[512,4096]{1,0:T(8,128)}) fusion(f32[512,4096]{1,0:T(8,128)} %copy-done.7, f32[512]{0:T(512)S(1)} %log_add_fusion, s32[512]{0:T(512)S(1)} %iota_add_fusion, s32[4096]{0:T(1024)S(1)} %convert_reduce_fusion, ...), kind=kOutput, calls=%fused_computation.7 | convolution fusion | flops 316667392 | bytes 84516864 | tf_op jit(solution)/shard_map/while/body/eval_jaxpr/dot_general | solution.py:56
  505.6 25.6 %multiply_reduce_fusion.1 = (f32[512]{0:T(512)S(1)}, f32[512]{0:T(512)S(1)}, f32[512]{0:T(512)S(1)}, bf16[512,4096]{1,0:T(8,128)(2,1)}, f32[512,4096]{1,0:T(8,128)}) fusion(f32[512,4096]{1,0:T(8,128)} %copy-done.4, f32[512]{0:T(512)S(1)} %get-tuple-element.145, s32[512]{0:T(512)S(1)} %iota_add_fusion, s32[4096]{0:T(1024)S(1)} %convert_reduce_fusion, ...), kind=kOutput, calls=%fused_computation.10 | convolution fusion | flops 310376960 | bytes 71929856 | tf_op jit(solution)/shard_map/while/body/eval_jaxpr/dot_general | solution.py:56
  531.2 21.3 %multiply_convert_fusion.2 = (bf16[512,4096]{1,0:T(8,128)(2,1)}, bf16[512,4096]{1,0:T(8,128)(2,1)}, bf16[512,4096]{1,0:T(8,128)(2,1)S(1)}) fusion(f32[512,4096]{1,0:T(8,128)} %fusion.78, f32[512]{0:T(512)S(1)} %get-tuple-element.88, f32[512,4096]{1,0:T(8,128)} %copy-done.8, f32[512]{0:T(512)S(1)} %get-tuple-element.146, s32[512]{0:T(512)S(1)} %iota_add_fusion, ...), kind=kLoop, calls=%fused_computation.12 | loop fusion | flops 37748736 | bytes 62947328 | tf_op jit(solution)/shard_map/while/body/eval_jaxpr/convert_element_type | solution.py:199
  556.3 27.1 %multiply_convert_fusion.1 = (bf16[512,4096]{1,0:T(8,128)(2,1)}, bf16[512,4096]{1,0:T(8,128)(2,1)}, bf16[512,4096]{1,0:T(8,128)(2,1)}, bf16[512,4096]{1,0:T(8,128)(2,1)}) fusion(f32[512,4096]{1,0:T(8,128)} %get-tuple-element.140, f32[512]{0:T(512)S(1)} %get-tuple-element.74, f32[512,4096]{1,0:T(8,128)} %copy-done.4, f32[512]{0:T(512)S(1)} %get-tuple-element.145, ...), kind=kLoop, calls=%fused_computation.9 | loop fusion | flops 48234496 | bytes 83922944 | tf_op jit(solution)/shard_map/while/body/eval_jaxpr/convert_element_type | solution.py:199
  583.4 3.2 fusion.145
  597.8 4.8 convolution_convert_fusion.3
  602.7 3.9 fusion.68
  606.7 3.7 fusion.67
  619.3 2.9 convolution_convert_fusion.4
  622.3 11.4 reduce-scatter.9.cloned.1.call-done
  637.0 10.0 convolution_convert_fusion.5
  649.0 3.0 fusion.180
  655.1 10.1 convolution_convert_fusion.1
  665.5 10.1 convolution_convert_fusion.2
  675.6 10.3 convolution_convert_fusion
  689.6 17.5 %reduce-scatter.11.cloned.1.call-done = bf16[256,512]{1,0:T(8,128)(2,1)} async-done(((bf16[2048,512]{1,0:T(8,128)(2,1)}), bf16[256,512]{1,0:T(8,128)(2,1)}) %reduce-scatter.11.cloned.1.call-update) | async-done | bytes 262160 | tf_op jit(solution)/shard_map/reduce_scatter | solution.py:244
  708.9 30.2 %reduce-scatter.13.cloned.1.call-done = bf16[256,128]{1,0:T(8,128)(2,1)} async-done(((bf16[2048,128]{1,0:T(8,128)(2,1)}), bf16[256,128]{1,0:T(8,128)(2,1)}) %reduce-scatter.13.cloned.1.call-update) | async-done | bytes 65552 | tf_op jit(solution)/shard_map/reduce_scatter | solution.py:247
  740.5 29.9 %reduce-scatter.15.cloned.1.call-done = bf16[256,128]{1,0:T(8,128)(2,1)} async-done(((bf16[2048,128]{1,0:T(8,128)(2,1)}), bf16[256,128]{1,0:T(8,128)(2,1)}) %reduce-scatter.15.cloned.1.call-update) | async-done | bytes 65552 | tf_op jit(solution)/shard_map/reduce_scatter | solution.py:250
  771.9 105.4 %all-reduce.9.cloned.1.call-done = (bf16[512,2048]{1,0:T(8,128)(2,1)}, bf16[512,2048]{1,0:T(8,128)(2,1)}) async-done(((bf16[512,2048]{1,0:T(8,128)(2,1)}, bf16[512,2048]{1,0:T(8,128)(2,1)}), (bf16[512,2048]{1,0:T(8,128)(2,1)}, bf16[512,2048]{1,0:T(8,128)(2,1)})) %all-reduce.9.cloned.1.call-update) | async-done | bytes 4194320 | tf_op jit(solution)/shard_map/psum | solution.py:169
  877.4 3.2 fusion.32
  880.6 17.4 %all-reduce.2 = (bf16[2048]{0:T(1024)(128)(2,1)S(1)}, bf16[2048]{0:T(1024)(128)(2,1)S(1)}) all-reduce(bf16[2048]{0:T(1024)(128)(2,1)S(1)} %get-tuple-element.67, bf16[2048]{0:T(1024)(128)(2,1)S(1)} %copy-done.52), channel_id=4, replica_groups=mesh['wide'=8,'narrow'=4] {'wide'}, use_global_device_ids=true, to_apply=%region_38.39.clone | all-reduce | flops 4096 | bytes 16384
  899.2 5.1 add_convert_fusion.2
  905.4 2.6 fusion.20
  908.0 61.6 %reduce-scatter.21.cloned.1.call-done = bf16[256,2048]{1,0:T(8,128)(2,1)} async-done(((bf16[2048,2048]{1,0:T(8,128)(2,1)}), bf16[256,2048]{1,0:T(8,128)(2,1)}) %reduce-scatter.21.cloned.1.call-update) | async-done | bytes 1048592 | tf_op jit(solution)/shard_map/reduce_scatter | solution.py:262
  969.6 2.8 convert_element_type.315
  972.4 87.4 %reduce-scatter.19.cloned.1.call-done = bf16[256,2048]{1,0:T(8,128)(2,1)} async-done(((bf16[2048,2048]{1,0:T(8,128)(2,1)}), bf16[256,2048]{1,0:T(8,128)(2,1)}) %reduce-scatter.19.cloned.1.call-update) | async-done | bytes 1048592 | tf_op jit(solution)/shard_map/reduce_scatter | solution.py:259
  1059.8 2.8 convert_element_type.313
  1062.6 87.3 %reduce-scatter.23.cloned.1.call-done = bf16[2048,256]{1,0:T(8,128)(2,1)} async-done(((bf16[2048,2048]{1,0:T(8,128)(2,1)}), bf16[2048,256]{1,0:T(8,128)(2,1)}) %reduce-scatter.23.cloned.1.call-update) | async-done | bytes 1048592 | tf_op jit(solution)/shard_map/reduce_scatter | solution.py:265
  1150.0 2.7 convert_element_type.317
  (282 shorter events, 99.7 us)
Async XLA Ops:
  7.2 124.0 %copy-start = (bf16[512,2048]{1,0:T(8,128)(2,1)S(1)}, bf16[512,2048]{1,0:T(8,128)(2,1)}, u32[]{:S(2)}) copy-start(bf16[512,2048]{1,0:T(8,128)(2,1)} %param.21) | copy-start | bytes 6291460
  7.2 7.9 copy-start.40
  7.2 42.6 %all-gather.4.cloned.1.call-start = ((), (), s32[]{:S(2)}) async-start(), calls=%async_computation.8 | async-start | bytes 2359296 | tf_op jit(solution)/shard_map/all_gather | solution.py:109
  10.1 9.4 copy-start.50
  10.9 4.2 copy-start.26
  12.5 6.9 copy-start.48
  12.5 3.6 copy-start.57
  17.0 6.0 copy-start.37
  17.9 273.7 %all-gather.6.cloned.1.call-start = ((), (), s32[]{:S(2)}) async-start(), calls=%async_computation.18 | async-start | bytes 20971520 | tf_op jit(solution)/shard_map/all_gather | solution.py:150
  19.3 409.9 %copy-start.53 = (pred[512]{0:T(512)(128)(4,1)}, pred[512]{0:T(512)(128)(4,1)S(1)}, u32[]{:S(2)}) copy-start(pred[512]{0:T(512)(128)(4,1)S(1)} %fusion.150) | copy-start | bytes 1540
  53.4 3.3 copy-start.7
  61.7 64.6 %copy-start.4 = (f32[512,4096]{1,0:T(8,128)}, f32[512,4096]{1,0:T(8,128)S(1)}, u32[]{:S(2)}) copy-start(f32[512,4096]{1,0:T(8,128)S(1)} %get-tuple-element.136) | copy-start | bytes 25165828
  89.0 25.9 %copy-start.5 = (f32[512,4096]{1,0:T(8,128)}, f32[512,4096]{1,0:T(8,128)S(1)}, u32[]{:S(2)}) copy-start(f32[512,4096]{1,0:T(8,128)S(1)} %get-tuple-element.128) | copy-start | bytes 25165828
  94.8 18.3 %copy-start.6 = (f32[512,4096]{1,0:T(8,128)}, f32[512,4096]{1,0:T(8,128)S(1)}, u32[]{:S(2)}) copy-start(f32[512,4096]{1,0:T(8,128)S(1)} %get-tuple-element.126) | copy-start | bytes 25165828
  103.2 4.8 copy-start.24
  114.9 7.2 slice-start.16
  116.7 5.4 slice-start.17
  116.7 7.2 slice-start.10
  124.4 3.7 slice-start.6
  131.2 3.4 copy-start.56
  134.5 286.2 %all-reduce.7.cloned.1.call-start = ((), (), s32[]{:S(2)}) async-start(), calls=%async_computation.9 | async-start | bytes 4194304 | tf_op jit(solution)/shard_map/psum | solution.py:171
  305.2 10.1 copy-start.2
  305.2 10.1 slice-start.22
  305.7 9.7 copy-start.35
  305.7 9.7 slice-start.23
  315.4 6.3 copy-start.36
  333.6 7.8 copy-start.59
  350.8 282.9 %reduce-scatter.9.cloned.1.call-start = ((), (), s32[]{:S(2)}) async-start(), calls=%async_computation.10 | async-start | bytes 2359296 | tf_op jit(solution)/shard_map/reduce_scatter | solution.py:221
  420.7 4.9 copy-start.3
  420.7 10.7 slice-start.14
  425.6 5.8 slice-start.15
  429.2 4.6 slice-start.18
  431.4 5.4 slice-start.4
  434.4 4.9 slice-start.2
  434.4 8.7 slice-start.20
  436.8 3.6 slice-start.3
  436.8 6.2 slice-start.21
  440.4 6.0 slice-start.12
  440.4 8.4 slice-start
  443.1 3.3 slice-start.13
  443.1 5.8 slice-start.1
  446.4 4.9 slice-start.8
  451.3 3.3 copy-start.25
  531.2 23.4 %copy-start.34 = (bf16[512,8,2,32]{0,3,2,1:T(8,128)(2,1)S(1)}, bf16[512,8,2,32]{0,3,2,1:T(8,128)(2,1)}, u32[]{:S(2)}) copy-start(bf16[512,8,2,32]{0,3,2,1:T(8,128)(2,1)} %pad_maximum_fusion.1) | copy-start | bytes 1572868
  583.4 3.5 copy-start.13
  583.4 3.7 copy-start.33
  597.8 90.0 %reduce-scatter.17.cloned.1.call-start = ((), (), s32[]{:S(2)}) async-start(), calls=%async_computation.14 | async-start | bytes 2359296 | tf_op jit(solution)/shard_map/reduce_scatter | solution.py:253
  602.7 104.4 %reduce-scatter.11.cloned.1.call-start = ((), (), s32[]{:S(2)}) async-start(), calls=%async_computation.11 | async-start | bytes 2359296 | tf_op jit(solution)/shard_map/reduce_scatter | solution.py:244
  602.7 7.7 copy-start.22
  606.6 5.2 copy-start.18
  619.3 15.4 %copy-start.28 = (bf16[512,2048]{1,0:T(8,128)(2,1)S(1)}, bf16[512,2048]{1,0:T(8,128)(2,1)}, u32[]{:S(2)}) copy-start(bf16[512,2048]{1,0:T(8,128)(2,1)} %param.16) | copy-start | bytes 6291460
  622.2 116.8 %reduce-scatter.13.cloned.1.call-start = ((), (), s32[]{:S(2)}) async-start(), calls=%async_computation.12 | async-start | bytes 589824 | tf_op jit(solution)/shard_map/reduce_scatter | solution.py:247
  636.6 133.9 %reduce-scatter.15.cloned.1.call-start = ((), (), s32[]{:S(2)}) async-start(), calls=%async_computation.13 | async-start | bytes 589824 | tf_op jit(solution)/shard_map/reduce_scatter | solution.py:250
  637.0 10.0 copy-start.47
  648.9 228.5 %all-reduce.9.cloned.1.call-start = ((), (), s32[]{:S(2)}) async-start(), calls=%async_computation.19 | async-start | bytes 8388608 | tf_op jit(solution)/shard_map/psum | solution.py:169
  655.1 314.5 %reduce-scatter.21.cloned.1.call-start = ((), (), s32[]{:S(2)}) async-start(), calls=%async_computation.16 | async-start | bytes 9437184 | tf_op jit(solution)/shard_map/reduce_scatter | solution.py:262
  665.3 394.6 %reduce-scatter.19.cloned.1.call-start = ((), (), s32[]{:S(2)}) async-start(), calls=%async_computation.15 | async-start | bytes 9437184 | tf_op jit(solution)/shard_map/reduce_scatter | solution.py:259
  675.6 474.4 %reduce-scatter.23.cloned.1.call-start = ((), (), s32[]{:S(2)}) async-start(), calls=%async_computation.17 | async-start | bytes 9437184 | tf_op jit(solution)/shard_map/reduce_scatter | solution.py:265
  685.9 194.6 %copy-start.52 = (bf16[2048]{0:T(1024)(128)(2,1)S(1)}, bf16[2048]{0:T(1024)(128)(2,1)}, u32[]{:S(2)}) copy-start(bf16[2048]{0:T(1024)(128)(2,1)} %get-tuple-element.65) | copy-start | bytes 12292
  707.1 197.2 %copy-start.55 = (f32[512]{0:T(512)S(1)}, f32[512]{0:T(512)}, u32[]{:S(2)}) copy-start(f32[512]{0:T(512)} %get-tuple-element.119) | copy-start | bytes 6148
  899.2 5.1 copy-start.29
  899.2 5.1 copy-start.31
  899.2 6.2 copy-start.32
  905.4 247.2 %copy-start.1 = (bf16[512,2048]{1,0:T(8,128)(2,1)S(1)}, bf16[512,2048]{1,0:T(8,128)(2,1)}, u32[]{:S(2)}) copy-start(bf16[512,2048]{1,0:T(8,128)(2,1)} %param.21) | copy-start | bytes 6291460
  (32 other events, 72.7 us)
Sparse Core Ops, SparseCore 0:
  18.0 31.7 all-gather.3
  134.6 156.8 all-gather.5
  351.0 69.6 all-reduce.6
  597.9 35.7 reduce-scatter.8
  635.9 34.4 reduce-scatter.16
  672.7 34.3 reduce-scatter.10
  709.4 29.5 reduce-scatter.12
  741.3 29.1 reduce-scatter.14
  774.9 102.4 all-reduce.8
  879.5 90.0 reduce-scatter.20
  971.9 87.8 reduce-scatter.18
  1062.0 87.9 reduce-scatter.22
